TPU v7x, 32 devices: a whole 2x2x4 slice. The times are simulated.
32 devices in a mesh: pipe: 2 (over core), row: 4 (over z), rep: 4 (over y, x).
Axes of the slice: x: 2, y: 2, z: 4, core: 2. Of those that a mesh axis runs over, the one named last changes fastest.
Arguments:
- features: bfloat16 [1, 4096, 256], P(None, ('pipe', 'row')), may hold values from -6 to 6
- tile_src: int32 [8, 4, 2, 12], P(('pipe', 'row'), 'rep'), may hold values from 0 to 7
- tile_dst: int32 [8, 4, 2, 12], P(('pipe', 'row'), 'rep'), may hold values from 0 to 7
- tile_count: int32 [8, 4, 2], P(('pipe', 'row'), 'rep'), may hold values from 1 to 12, as said below
- edge_dst: int32 [8, 4, 2, 12, 256], P(('pipe', 'row'), 'rep'), may hold values from 0 to 63
- edge_src: int32 [8, 4, 2, 12, 256], P(('pipe', 'row'), 'rep'), may hold values from 0 to 63
- edge_weight: float32 [8, 4, 2, 12, 256], P(('pipe', 'row'), 'rep'), may hold values from 0.25 to 4
- w_msg: bfloat16 [2, 256, 256], replicated, may hold values from -0.375 to 0.375
- w_self: bfloat16 [2, 256, 256], replicated, may hold values from -0.375 to 0.375
- w_mid: bfloat16 [2, 256, 256], replicated, may hold values from -0.375 to 0.375
- w_out: bfloat16 [2, 256, 256], replicated, may hold values from -0.375 to 0.375
- gain: float32 [2, 256], replicated, may hold values from 0.1 to 1.9
Outputs:
- hidden: bfloat16 [2, 1, 4096, 256], P(None, None, ('pipe', 'row'))
Inputs may be any that keep to these rules, and one draw needn't show every extreme that they name: `tile_count`: every entry is at least 1 and at most 12; for every row block and every index of rep, some section has exactly 12 live slots.
All inputs are finite; a program needn't handle non-finite values.
Results may differ from a plain program's by a relative error of at most 0.0054.
Values may be sent and summed in bfloat16 or wider, within the bound.
A program may use at most 64 MiB of HBM per device.

v0:
```python
import jax
import jax.numpy as jnp
from jax import lax
from jax.sharding import PartitionSpec as P

BS = 64
LAYERS = 2


def build_tiles(dst, src, weight):
    hot_dst = (dst[..., None] == jnp.arange(BS)).astype(jnp.float32) * weight[..., None]
    hot_src = (src[..., None] == jnp.arange(BS)).astype(jnp.float32)
    made = jnp.einsum("...ea,...eb->...ab", hot_dst, hot_src, precision=lax.Precision.HIGHEST)
    return made.astype(jnp.bfloat16)


def section_product(source, tiles_now, src_now, hot_now):
    rows, width = source.shape
    blocked = source.reshape(rows // BS, BS, width)
    picked = jnp.take(blocked, src_now, axis=0)
    prod = jnp.einsum("kab,kbf->kaf", tiles_now, picked, preferred_element_type=jnp.float32)
    summed = jnp.einsum("kn,kaf->naf", hot_now, prod, precision=lax.Precision.HIGHEST)
    return summed.reshape(rows, width)


def update_rows(rows_in, summed, wself, wmid, wout, gain_row):
    stat = jnp.mean(summed * summed, axis=-1, keepdims=True)
    normed = summed * lax.rsqrt(stat + 1e-05) * gain_row
    pre = jnp.dot(rows_in, wself, preferred_element_type=jnp.float32) + normed
    first = jax.nn.silu(pre).astype(jnp.bfloat16)
    second = jax.nn.silu(jnp.dot(first, wmid, preferred_element_type=jnp.float32)).astype(
        jnp.bfloat16
    )
    return (
        rows_in.astype(jnp.float32) + jnp.dot(second, wout, preferred_element_type=jnp.float32)
    ).astype(jnp.bfloat16)


def on_device(
    features,
    tile_src,
    tile_dst,
    tile_count,
    edge_dst,
    edge_src,
    edge_weight,
    w_msg,
    w_self,
    w_mid,
    w_out,
    gain,
):
    events, rows, width = features.shape
    blocks = rows // BS
    slots = tile_src.shape[3]
    rep_count = lax.axis_size("rep")
    my_rep = lax.axis_index("rep")
    quarter = width // rep_count
    tiles = build_tiles(edge_dst[0, 0], edge_src[0, 0], edge_weight[0, 0])
    live_int = (jnp.arange(slots)[None, :] < tile_count[0, 0][:, None]).astype(jnp.int32)
    src_idx = tile_src[0, 0]
    dst_idx = tile_dst[0, 0]
    tiles_all = lax.all_gather(tiles[None], "rep", axis=0, tiled=True)
    index_all = lax.all_gather(
        jnp.stack([src_idx, dst_idx, live_int])[None], "rep", axis=0, tiled=True
    )
    results = []
    for level in range(LAYERS):
        results.append([])
    state = features[0]
    for level in range(LAYERS):
        wmsg = w_msg[level]
        wself = w_self[level]
        wmid = w_mid[level]
        wout = w_out[level]
        gain_row = gain[level]
        y = jnp.dot(state, wmsg, preferred_element_type=jnp.float32).astype(jnp.bfloat16)
        y_share = lax.dynamic_slice_in_dim(y, my_rep * quarter, quarter, 1)
        piece = lax.all_gather(y_share, ("pipe", "row"), axis=0, tiled=True)
        count = piece.shape[0] // rows

        def one_block(i, acc):
            owner_rep = i % rep_count
            section = i // rep_count
            tiles_rep = lax.dynamic_index_in_dim(tiles_all, owner_rep, 0, keepdims=False)
            tiles_now = lax.dynamic_index_in_dim(tiles_rep, section, 0, keepdims=False)
            info_rep = lax.dynamic_index_in_dim(index_all, owner_rep, 0, keepdims=False)
            info = lax.dynamic_index_in_dim(info_rep, section, 1, keepdims=False)
            hot_now = (info[1][:, None] == jnp.arange(blocks)).astype(jnp.float32) * info[2].astype(
                jnp.float32
            )[:, None]
            sub = lax.dynamic_slice_in_dim(piece, i * rows, rows, 0)
            return acc + section_product(sub, tiles_now, info[0], hot_now)

        column_sum = lax.fori_loop(0, count, one_block, jnp.zeros((rows, quarter), jnp.float32))
        summed = lax.all_gather(column_sum, "rep", axis=1, tiled=True)
        state = update_rows(state, summed, wself, wmid, wout, gain_row)
        results[level].append(state)
    return jnp.stack([jnp.stack(items) for items in results])


def solution(mesh):
    placed = (
        P(None, ("pipe", "row"), None),
        P(("pipe", "row"), "rep", None, None),
        P(("pipe", "row"), "rep", None, None),
        P(("pipe", "row"), "rep", None),
        P(("pipe", "row"), "rep", None, None, None),
        P(("pipe", "row"), "rep", None, None, None),
        P(("pipe", "row"), "rep", None, None, None),
        P(),
        P(),
        P(),
        P(),
        P(),
    )
    return jax.shard_map(
        on_device,
        mesh=mesh,
        in_specs=placed,
        out_specs=P(None, None, ("pipe", "row"), None),
        check_vma=False,
    )
```

profile of v0, /device:TPU:0, one launch (start us, length us, event | category | flops | bytes accessed | tf_op | source)
XLA Modules:
  0.0 140.6 jit_solution(12819187617356729768)
XLA Ops:
  0.0 1.2 fusion.56
  1.3 27.9 %all_gather.20 = bf16[4096,64]{0,1:T(8,128)(2,1)S(1)} all-gather(bf16[512,64]{0,1:T(8,128)(2,1)S(1)} %dynamic-slice_convert_fusion.1), channel_id=1, replica_groups=mesh['pipe'=2,'row'=4,'rep'=4] {'pipe','row'}, dimensions={0}, use_global_device_ids=true | all-gather | bytes 589824 | tf_op jit(solution)/shard_map/all_gather | solution.py:79
  29.2 0.7 copy.31
  29.9 0.7 copy.32
  30.6 0.7 copy.33
  31.4 1.2 fusion.40
  32.6 18.9 %all-gather.1 = bf16[8,12,64,64]{3,2,1,0:T(8,128)(2,1)S(1)} all-gather(bf16[2,12,64,64]{3,2,1,0:T(8,128)(2,1)S(1)} %fusion.40), channel_id=3, replica_groups=mesh['pipe'=2,'row'=4,'rep'=4] {'rep'}, dimensions={0}, use_global_device_ids=true | all-gather | bytes 983040 | tf_op jit(solution)/shard_map/all_gather | solution.py:63
  51.6 8.3 %all-gather = s32[12,2,12]{2,1,0:T(2,128)S(1)} all-gather(s32[3,2,12]{2,1,0:T(2,128)S(1)} %pad_add_fusion), channel_id=2, replica_groups=mesh['pipe'=2,'row'=4,'rep'=4] {'rep'}, dimensions={0}, use_global_device_ids=true | all-gather | bytes 1440 | tf_op jit(solution)/shard_map/all_gather | solution.py:64
  59.9 15.6 %while.34 = (s32[]{:T(128)}, f32[512,64]{0,1:T(8,128)S(1)}, s32[4,3,2,12]{3,2,1,0:T(2,128)S(1)}, bf16[4,2,12,64,64]{4,3,2,1,0:T(8,128)(2,1)S(1)}, bf16[4096,64]{...) while((s32[]{:T(128)}, f32[512,64]{0,1:T(8,128)S(1)}, ...), condition=%wide.region_1.3_spmd.clone, body=%wide.region_0.2_spmd.clone.sunk | while | flops 11126065 | bytes 2430404 | solution.py:95
  60.1 0.6 gather_fusion
  62.1 0.6 gather_fusion
  64.0 0.6 gather_fusion
  66.0 0.6 gather_fusion
  67.9 0.6 gather_fusion
  69.9 0.6 gather_fusion
  71.8 0.6 gather_fusion
  73.8 0.6 gather_fusion
  75.6 9.3 %all_gather.21 = f32[512,256]{0,1:T(8,128)S(1)} all-gather(f32[512,64]{0,1:T(8,128)S(1)} %get-tuple-element.330), channel_id=1, replica_groups=mesh['pipe'=2,'row'=4,'rep'=4] {'rep'}, dimensions={1}, use_global_device_ids=true | all-gather | bytes 655360 | tf_op jit(solution)/shard_map/all_gather | solution.py:96
  85.2 1.4 multiply_convert_fusion.2
  87.2 26.4 %all_gather.22 = bf16[4096,64]{0,1:T(8,128)(2,1)S(1)} all-gather(bf16[512,64]{0,1:T(8,128)(2,1)S(1)} %dynamic-slice_convert_fusion), channel_id=1, replica_groups=mesh['pipe'=2,'row'=4,'rep'=4] {'pipe','row'}, dimensions={0}, use_global_device_ids=true | all-gather | bytes 589824 | tf_op jit(solution)/shard_map/all_gather | solution.py:79
  113.6 15.5 %while.35 = (s32[]{:T(128)}, f32[512,64]{0,1:T(8,128)S(1)}, s32[4,3,2,12]{3,2,1,0:T(2,128)S(1)}, bf16[4,2,12,64,64]{4,3,2,1,0:T(8,128)(2,1)S(1)}, bf16[4096,64]{...) while((s32[]{:T(128)}, f32[512,64]{0,1:T(8,128)S(1)}, ...), condition=%wide.region_4.6_spmd.clone, body=%wide.region_3.5_spmd.clone.sunk | while | flops 11126065 | bytes 2430404 | solution.py:95
  113.8 0.6 gather_fusion.1
  129.2 9.1 %all_gather.23 = f32[512,256]{0,1:T(8,128)S(1)} all-gather(f32[512,64]{0,1:T(8,128)S(1)} %get-tuple-element.331), channel_id=1, replica_groups=mesh['pipe'=2,'row'=4,'rep'=4] {'rep'}, dimensions={1}, use_global_device_ids=true | all-gather | bytes 655360 | tf_op jit(solution)/shard_map/all_gather | solution.py:96
  139.8 0.8 pad_maximum_fusion
  (206 shorter events, 26.4 us)
Async XLA Ops:
  31.4 20.1 %copy-start.10 = (s32[1,1,2]{2,1,0:T(1,128)S(1)}, s32[1,1,2]{2,1,0:T(1,128)}, u32[]{:S(2)}) copy-start(s32[1,1,2]{2,1,0:T(1,128)} %param.21) | copy-start | bytes 28
  31.4 20.2 %copy-start.5 = (s32[1,1,2,12]{3,2,1,0:T(2,128)S(1)}, s32[1,1,2,12]{3,2,1,0:T(2,128)}, u32[]{:S(2)}) copy-start(s32[1,1,2,12]{3,2,1,0:T(2,128)} %param.20) | copy-start | bytes 292
  31.4 20.2 %copy-start.6 = (s32[1,1,2,12]{3,2,1,0:T(2,128)S(1)}, s32[1,1,2,12]{3,2,1,0:T(2,128)}, u32[]{:S(2)}) copy-start(s32[1,1,2,12]{3,2,1,0:T(2,128)} %param.19) | copy-start | bytes 292
  75.5 9.6 %copy-start.4 = (f32[2,256]{1,0:T(2,128)S(1)}, f32[2,256]{1,0:T(2,128)}, u32[]{:S(2)}) copy-start(f32[2,256]{1,0:T(2,128)} %param.29) | copy-start | bytes 6148
  75.5 9.6 %copy-start = (bf16[1,512,256]{2,1,0:T(8,128)(2,1)S(1)}, bf16[1,512,256]{2,1,0:T(8,128)(2,1)}, u32[]{:S(2)}) copy-start(bf16[1,512,256]{2,1,0:T(8,128)(2,1)} %param.18) | copy-start | bytes 786436
  75.6 9.6 %copy-start.7 = (bf16[2,256,256]{2,1,0:T(8,128)(2,1)S(1)}, bf16[2,256,256]{2,1,0:T(8,128)(2,1)}, u32[]{:S(2)}) copy-start(bf16[2,256,256]{2,1,0:T(8,128)(2,1)} %param.27) | copy-start | bytes 786436
  85.2 1.4 %copy-start.2 = (bf16[2,256,256]{2,1,0:T(8,128)(2,1)S(1)}, bf16[2,256,256]{2,1,0:T(8,128)(2,1)}, u32[]{:S(2)}) copy-start(bf16[2,256,256]{2,1,0:T(8,128)(2,1)} %param.28) | copy-start | bytes 786436
  85.2 1.7 %copy-start.1 = (bf16[2,256,256]{2,1,0:T(8,128)(2,1)S(1)}, bf16[2,256,256]{2,1,0:T(8,128)(2,1)}, u32[]{:S(2)}) copy-start(bf16[2,256,256]{2,1,0:T(8,128)(2,1)} %param.25) | copy-start | bytes 786436
  129.1 9.4 %copy-start.8 = (bf16[2,256,256]{2,1,0:T(8,128)(2,1)S(1)}, bf16[2,256,256]{2,1,0:T(8,128)(2,1)}, u32[]{:S(2)}) copy-start(bf16[2,256,256]{2,1,0:T(8,128)(2,1)} %param.27) | copy-start | bytes 786436
  129.1 9.4 %copy-start.9 = (bf16[2,256,256]{2,1,0:T(8,128)(2,1)S(1)}, bf16[2,256,256]{2,1,0:T(8,128)(2,1)}, u32[]{:S(2)}) copy-start(bf16[2,256,256]{2,1,0:T(8,128)(2,1)} %param.26) | copy-start | bytes 786436
  138.6 1.0 copy-start.3
where the time goes:
time: 141 us
  blocking collectives  100 us (71%)
  local copies, waits for them, and re-layouts  20.9 us (15%)
  matrix products  15.4 us (11%)
  other arithmetic  2.33 us (2%)
  loops' own time  1.8 us (1%)
    all_gather x2, blocking collectives, on_device(): piece = lax.all_gather(y_share, ('pipe', 'row'), axis=0, tiled=True)  54.3 us
    all_gather x1, blocking collectives, on_device(): tiles_all = lax.all_gather(tiles[None], 'rep', axis=0, tiled=True)  18.9 us
    all_gather x2, blocking collectives, on_device(): summed = lax.all_gather(column_sum, 'rep', axis=1, tiled=True)  18.4 us
    gather x16, local copies, waits for them, and re-layouts, section_product(): picked = jnp.take(blocked, src_now, axis=0)  9.42 us
    all_gather x1, blocking collectives, on_device(): lax.all_gather(jnp.stack([src_idx, dst_idx, live_int])[None], 'rep', axis...  8.33 us
    dot_general x16, matrix products, section_product(): jnp.einsum('kn,kaf->naf', hot_now, prod, precision=lax.Precision.HIGHEST)  6.06 us
    dot_general x16, local copies, waits for them, and re-layouts, section_product(): jnp.einsum('kab,kbf->kaf', tiles_now, picked, preferred_element_type=jnp....  4.37 us
    dot_general x16, matrix products, section_product(): jnp.einsum('kab,kbf->kaf', tiles_now, picked, preferred_element_type=jnp....  4.28 us

commit v1 on v0

--- a/solution.py
+++ b/solution.py
@@ -2,6 +2,7 @@
 import jax.numpy as jnp
 from jax import lax
 from jax.sharding import PartitionSpec as P
+from jax.lax import axis_index, axis_size, ppermute
 
 BS = 64
 LAYERS = 2
@@ -76,7 +77,17 @@
         gain_row = gain[level]
         y = jnp.dot(state, wmsg, preferred_element_type=jnp.float32).astype(jnp.bfloat16)
         y_share = lax.dynamic_slice_in_dim(y, my_rep * quarter, quarter, 1)
-        piece = lax.all_gather(y_share, ("pipe", "row"), axis=0, tiled=True)
+        y_new, val2 = (axis_size(("pipe", "row")), axis_index(("pipe", "row")))
+        piece, now = (y_share, 1)
+        while now < y_new:
+            all_rows = []
+            for w in [*range(y_new)]:
+                all_rows.append((w, w ^ now))
+            piece_next = ppermute(piece, axis_name=("pipe", "row"), perm=all_rows)
+            state_next = jnp.concatenate([piece, piece_next], axis=0)
+            field_out = jnp.concatenate([piece_next, piece], axis=0)
+            piece = jnp.where(val2 & now == 0, state_next, field_out)
+            now = 2 * now
         count = piece.shape[0] // rows
 
         def one_block(i, acc):

time: 141 us -> 105 us (0.74)
  blocking collectives: 100 us -> 44.5 us
  waiting for transfers between devices: 0 us -> 12.1 us
  starting transfers between devices: 0 us -> 7.08 us
    all_gather x2 -> x0, blocking collectives: 54.3 us -> none  [on_device(): piece = lax.all_gather(y_share, ('pipe', 'row'), axis=0, tiled=True)]
    ppermute x0 -> x6, waiting for transfers between devices: none -> 12.1 us  [on_device(): piece_next = ppermute(piece, axis_name=('pipe', 'row'), perm=all_rows)]
    ppermute x0 -> x6, starting transfers between devices: none -> 7.08 us  [on_device(): piece_next = ppermute(piece, axis_name=('pipe', 'row'), perm=all_rows)]
    all_gather x1, blocking collectives: 18.9 us -> 16.8 us  [on_device(): tiles_all = lax.all_gather(tiles[None], 'rep', axis=0, tiled=True)]
  transfers between devices with their start and end apart: 0 -> 6, of which waited for: 0 -> 3; matrix products, arithmetic and copies ran while one was open for 0% -> 3% of each run, Pallas kernels for 0% -> 0%
where the time goes in v1:
time: 105 us
  blocking collectives  44.5 us (42%)
  local copies, waits for them, and re-layouts  20.9 us (20%)
  matrix products  15.4 us (15%)
  waiting for transfers between devices  12.1 us (12%)
  starting transfers between devices  7.08 us (7%)
  other arithmetic  2.8 us (3%)
  loops' own time  1.86 us (2%)
    all_gather x2, blocking collectives, on_device(): summed = lax.all_gather(column_sum, 'rep', axis=1, tiled=True)  19.7 us
    all_gather x1, blocking collectives, on_device(): tiles_all = lax.all_gather(tiles[None], 'rep', axis=0, tiled=True)  16.8 us
    ppermute x6, waiting for transfers between devices, on_device(): piece_next = ppermute(piece, axis_name=('pipe', 'row'), perm=all_rows)  12.1 us
    gather x16, local copies, waits for them, and re-layouts, section_product(): picked = jnp.take(blocked, src_now, axis=0)  9.41 us
    all_gather x1, blocking collectives, on_device(): lax.all_gather(jnp.stack([src_idx, dst_idx, live_int])[None], 'rep', axis...  7.95 us
    ppermute x6, starting transfers between devices, on_device(): piece_next = ppermute(piece, axis_name=('pipe', 'row'), perm=all_rows)  7.08 us
    dot_general x16, matrix products, section_product(): jnp.einsum('kn,kaf->naf', hot_now, prod, precision=lax.Precision.HIGHEST)  6.05 us
    dot_general x16, local copies, waits for them, and re-layouts, section_product(): jnp.einsum('kab,kbf->kaf', tiles_now, picked, preferred_element_type=jnp....  4.37 us
  transfers between devices with their start and end apart: 6, of which 3 were waited for; matrix products, arithmetic and copies ran while one was open for 3% of the time, Pallas kernels for 0%

profile of v1, /device:TPU:0, one launch (start us, length us, event | category | flops | bytes accessed | tf_op | source)
XLA Modules:
  0.0 105.0 jit_solution(17615854771820416448)
XLA Ops:
  0.0 1.3 %fusion.56 = bf16[512,256]{0,1:T(8,128)(2,1)S(1)} fusion(bf16[1,512,256]{2,1,0:T(8,128)(2,1)} %param.18, bf16[2,256,256]{2,1,0:T(8,128)(2,1)} %param.25), kind=kOutput, calls=%fused_computation.91 | convolution fusion | flops 67108864 | bytes 655360 | tf_op jit(solution)/shard_map/dot_general | solution.py:78
  1.3 3.1 %collective-permute-start = (bf16[512,64]{0,1:T(8,128)(2,1)S(1)}, bf16[512,64]{0,1:T(8,128)(2,1)S(1)}, u32[]{:S(2)}, u32[]{:S(2)}) collective-permute-start(bf16[512,64]{0,1:T(8,128)(2,1)S(1)} %dynamic-slice_convert_fusion.1), channel_id=1, source_target_pairs={{0,4},{4,0},{8,12},{12,8},{16,20},{20,16},{24,28},{28,24},{1,5},{5... | collective-permute-start | bytes 196616 | tf_op jit(solution)/shard_map/ppermute | solution.py:86
  4.4 0.7 copy.31
  5.2 0.7 copy.32
  5.9 0.7 copy.33
  6.6 1.2 %fusion.40 = bf16[2,12,64,64]{3,2,1,0:T(8,128)(2,1)S(1)} fusion(s32[2,12,256]{2,1,0:T(8,128)S(1)} %copy.33, f32[2,12,256]{2,1,0:T(8,128)S(1)} %copy.32, s32[2,12,256]{2,1,0:T(8,128)S(1)} %copy.31), kind=kOutput, calls=%fused_computation.62 | convolution fusion | flops 303267840 | bytes 270336 | tf_op jit(solution)/shard_map/...ea,...eb->...ab/dot_general | solution.py:14
  8.0 2.7 %collective-permute-start.1 = (bf16[1024,64]{0,1:T(8,128)(2,1)S(1)}, bf16[1024,64]{0,1:T(8,128)(2,1)S(1)}, u32[]{:S(2)}, u32[]{:S(2)}) collective-permute-start(bf16[1024,64]{0,1:T(8,128)(2,1)S(1)} %maximum_select_fusion.4), channel_id=1, source_target_pairs={{0,8},{4,12},{8,0},{12,4},{16,24},{20,28},{24,16},{28,20},{1,9},{5... | collective-permute-start | bytes 393224 | tf_op jit(solution)/shard_map/ppermute | solution.py:86
  10.7 16.8 %all-gather.1 = bf16[8,12,64,64]{3,2,1,0:T(8,128)(2,1)S(1)} all-gather(bf16[2,12,64,64]{3,2,1,0:T(8,128)(2,1)S(1)} %fusion.40), channel_id=3, replica_groups=mesh['pipe'=2,'row'=4,'rep'=4] {'rep'}, dimensions={0}, use_global_device_ids=true | all-gather | bytes 983040 | tf_op jit(solution)/shard_map/all_gather | solution.py:64
  27.7 8.0 %all-gather = s32[12,2,12]{2,1,0:T(2,128)S(1)} all-gather(s32[3,2,12]{2,1,0:T(2,128)S(1)} %pad_add_fusion), channel_id=2, replica_groups=mesh['pipe'=2,'row'=4,'rep'=4] {'rep'}, dimensions={0}, use_global_device_ids=true | all-gather | bytes 1440 | tf_op jit(solution)/shard_map/all_gather | solution.py:65
  35.8 15.6 %while.34 = (s32[]{:T(128)}, f32[512,64]{0,1:T(8,128)S(1)}, s32[4,3,2,12]{3,2,1,0:T(2,128)S(1)}, bf16[4,2,12,64,64]{4,3,2,1,0:T(8,128)(2,1)S(1)}, bf16[4096,64]{...) while((s32[]{:T(128)}, f32[512,64]{0,1:T(8,128)S(1)}, ...), condition=%wide.region_1.3_spmd.clone, body=%wide.region_0.2_spmd.clone.sunk | while | flops 11126065 | bytes 2430404 | solution.py:106
  36.0 0.6 gather_fusion
  37.9 0.6 gather_fusion
  39.9 0.6 gather_fusion
  47.7 0.6 gather_fusion
  51.3 9.9 %all_gather.14 = f32[512,256]{0,1:T(8,128)S(1)} all-gather(f32[512,64]{0,1:T(8,128)S(1)} %get-tuple-element.330), channel_id=1, replica_groups=mesh['pipe'=2,'row'=4,'rep'=4] {'rep'}, dimensions={1}, use_global_device_ids=true | all-gather | bytes 655360 | tf_op jit(solution)/shard_map/all_gather | solution.py:107
  61.6 1.5 %multiply_convert_fusion.2 = bf16[512,256]{1,0:T(8,128)(2,1)S(1)} fusion(f32[512,256]{1,0:T(8,128)S(1)} %copy.35, bf16[1,512,256]{2,1,0:T(8,128)(2,1)S(1)} %copy-done, f32[256]{0:T(256)S(1)} %bitcast.119, f32[512]{0:T(512)S(1)} %add_rsqrt_fusion.1, bf16[2,256,256]{2,1,0:T(8,128)(2,1)} %param.27, bf16[2,256,256]{2,1,0:T(8,128)(2,1)} %param.26), kind=kOutput, calls=%fused_computation.83 | convolution fusion | flops 135921664 | bytes 1313792 | tf_op jit(solution)/shard_map/dot_general | solution.py:32
  63.6 0.7 collective-permute-start.3
  64.3 4.3 %collective-permute-done.3 = bf16[512,64]{0,1:T(8,128)(2,1)S(1)} collective-permute-done((bf16[512,64]{0,1:T(8,128)(2,1)S(1)}, bf16[512,64]{0,1:T(8,128)(2,1)S(1)}, u32[]{:S(2)}, u32[]{:S(2)}) %collective-permute-start.3) | collective-permute-done | bytes 65568 | tf_op jit(solution)/shard_map/ppermute | solution.py:86
  69.1 6.3 %collective-permute-done.4 = bf16[1024,64]{0,1:T(8,128)(2,1)S(1)} collective-permute-done((bf16[1024,64]{0,1:T(8,128)(2,1)S(1)}, bf16[1024,64]{0,1:T(8,128)(2,1)S(1)}, u32[]{:S(2)}, u32[]{:S(2)}) %collective-permute-start.4) | collective-permute-done | bytes 131104 | tf_op jit(solution)/shard_map/ppermute | solution.py:86
  75.6 1.5 %collective-permute-done.5 = bf16[2048,64]{0,1:T(8,128)(2,1)S(1)} collective-permute-done((bf16[2048,64]{0,1:T(8,128)(2,1)S(1)}, bf16[2048,64]{0,1:T(8,128)(2,1)S(1)}, u32[]{:S(2)}, u32[]{:S(2)}) %collective-permute-start.5) | collective-permute-done | bytes 262176 | tf_op jit(solution)/shard_map/ppermute | solution.py:86
  77.2 15.6 %while.35 = (s32[]{:T(128)}, f32[512,64]{0,1:T(8,128)S(1)}, s32[4,3,2,12]{3,2,1,0:T(2,128)S(1)}, bf16[4,2,12,64,64]{4,3,2,1,0:T(8,128)(2,1)S(1)}, bf16[4096,64]{...) while((s32[]{:T(128)}, f32[512,64]{0,1:T(8,128)S(1)}, ...), condition=%wide.region_4.6_spmd.clone, body=%wide.region_3.5_spmd.clone.sunk | while | flops 11126065 | bytes 2430404 | solution.py:106
  87.2 0.6 gather_fusion.1
  92.9 9.8 %all_gather.15 = f32[512,256]{0,1:T(8,128)S(1)} all-gather(f32[512,64]{0,1:T(8,128)S(1)} %get-tuple-element.331), channel_id=1, replica_groups=mesh['pipe'=2,'row'=4,'rep'=4] {'rep'}, dimensions={1}, use_global_device_ids=true | all-gather | bytes 655360 | tf_op jit(solution)/shard_map/all_gather | solution.py:107
  104.1 0.8 pad_maximum_fusion
  (220 shorter events, 29.9 us)
Async XLA Ops:
  0.0 7.9 %copy-start.9 = (s32[1,1,2]{2,1,0:T(1,128)S(1)}, s32[1,1,2]{2,1,0:T(1,128)}, u32[]{:S(2)}) copy-start(s32[1,1,2]{2,1,0:T(1,128)} %param.21) | copy-start | bytes 28
  1.3 6.7 %collective-permute-start = (bf16[512,64]{0,1:T(8,128)(2,1)S(1)}, bf16[512,64]{0,1:T(8,128)(2,1)S(1)}, u32[]{:S(2)}, u32[]{:S(2)}) collective-permute-start(bf16[512,64]{0,1:T(8,128)(2,1)S(1)} %dynamic-slice_convert_fusion.1), channel_id=1, source_target_pairs={{0,4},{4,0},{8,12},{12,8},{16,20},{20,16},{24,28},{28,24},{1,5},{5... | collective-permute-start | bytes 196616 | tf_op jit(solution)/shard_map/ppermute | solution.py:86
  7.8 19.8 %copy-start.5 = (s32[1,1,2,12]{3,2,1,0:T(2,128)S(1)}, s32[1,1,2,12]{3,2,1,0:T(2,128)}, u32[]{:S(2)}) copy-start(s32[1,1,2,12]{3,2,1,0:T(2,128)} %param.20) | copy-start | bytes 292
  7.9 19.8 %copy-start.6 = (s32[1,1,2,12]{3,2,1,0:T(2,128)S(1)}, s32[1,1,2,12]{3,2,1,0:T(2,128)}, u32[]{:S(2)}) copy-start(s32[1,1,2,12]{3,2,1,0:T(2,128)} %param.19) | copy-start | bytes 292
  7.9 27.7 %copy-start.4 = (f32[2,256]{1,0:T(2,128)S(1)}, f32[2,256]{1,0:T(2,128)}, u32[]{:S(2)}) copy-start(f32[2,256]{1,0:T(2,128)} %param.29) | copy-start | bytes 6148
  8.0 19.4 %collective-permute-start.1 = (bf16[1024,64]{0,1:T(8,128)(2,1)S(1)}, bf16[1024,64]{0,1:T(8,128)(2,1)S(1)}, u32[]{:S(2)}, u32[]{:S(2)}) collective-permute-start(bf16[1024,64]{0,1:T(8,128)(2,1)S(1)} %maximum_select_fusion.4), channel_id=1, source_target_pairs={{0,8},{4,12},{8,0},{12,4},{16,24},{20,28},{24,16},{28,20},{1,9},{5... | collective-permute-start | bytes 393224 | tf_op jit(solution)/shard_map/ppermute | solution.py:86
  27.5 8.1 %collective-permute-start.2 = (bf16[2048,64]{0,1:T(8,128)(2,1)S(1)}, bf16[2048,64]{0,1:T(8,128)(2,1)S(1)}, u32[]{:S(2)}, u32[]{:S(2)}) collective-permute-start(bf16[2048,64]{0,1:T(8,128)(2,1)S(1)} %maximum_select_fusion.2), channel_id=1, source_target_pairs={{0,16},{4,20},{8,24},{12,28},{16,0},{20,4},{24,8},{28,12},{1,17},{... | collective-permute-start | bytes 786440 | tf_op jit(solution)/shard_map/ppermute | solution.py:86
  51.3 10.2 %copy-start = (bf16[1,512,256]{2,1,0:T(8,128)(2,1)S(1)}, bf16[1,512,256]{2,1,0:T(8,128)(2,1)}, u32[]{:S(2)}) copy-start(bf16[1,512,256]{2,1,0:T(8,128)(2,1)} %param.18) | copy-start | bytes 786436
  61.6 1.5 %copy-start.2 = (bf16[2,256,256]{2,1,0:T(8,128)(2,1)S(1)}, bf16[2,256,256]{2,1,0:T(8,128)(2,1)}, u32[]{:S(2)}) copy-start(bf16[2,256,256]{2,1,0:T(8,128)(2,1)} %param.28) | copy-start | bytes 786436
  61.6 1.7 %copy-start.1 = (bf16[2,256,256]{2,1,0:T(8,128)(2,1)S(1)}, bf16[2,256,256]{2,1,0:T(8,128)(2,1)}, u32[]{:S(2)}) copy-start(bf16[2,256,256]{2,1,0:T(8,128)(2,1)} %param.25) | copy-start | bytes 786436
  63.6 4.9 %collective-permute-start.3 = (bf16[512,64]{0,1:T(8,128)(2,1)S(1)}, bf16[512,64]{0,1:T(8,128)(2,1)S(1)}, u32[]{:S(2)}, u32[]{:S(2)}) collective-permute-start(bf16[512,64]{0,1:T(8,128)(2,1)S(1)} %dynamic-slice_convert_fusion), channel_id=1, source_target_pairs={{0,4},{4,0},{8,12},{12,8},{16,20},{20,16},{24,28},{28,24},{1,5},{5... | collective-permute-start | bytes 196616 | tf_op jit(solution)/shard_map/ppermute | solution.py:86
  68.6 6.8 %collective-permute-start.4 = (bf16[1024,64]{0,1:T(8,128)(2,1)S(1)}, bf16[1024,64]{0,1:T(8,128)(2,1)S(1)}, u32[]{:S(2)}, u32[]{:S(2)}) collective-permute-start(bf16[1024,64]{0,1:T(8,128)(2,1)S(1)} %maximum_select_fusion.5), channel_id=1, source_target_pairs={{0,8},{4,12},{8,0},{12,4},{16,24},{20,28},{24,16},{28,20},{1,9},{5... | collective-permute-start | bytes 393224 | tf_op jit(solution)/shard_map/ppermute | solution.py:86
  75.5 1.6 %collective-permute-start.5 = (bf16[2048,64]{0,1:T(8,128)(2,1)S(1)}, bf16[2048,64]{0,1:T(8,128)(2,1)S(1)}, u32[]{:S(2)}, u32[]{:S(2)}) collective-permute-start(bf16[2048,64]{0,1:T(8,128)(2,1)S(1)} %maximum_select_fusion.3), channel_id=1, source_target_pairs={{0,16},{4,20},{8,24},{12,28},{16,0},{20,4},{24,8},{28,12},{1,17},{... | collective-permute-start | bytes 786440 | tf_op jit(solution)/shard_map/ppermute | solution.py:86
  92.8 10.1 %copy-start.7 = (bf16[2,256,256]{2,1,0:T(8,128)(2,1)S(1)}, bf16[2,256,256]{2,1,0:T(8,128)(2,1)}, u32[]{:S(2)}) copy-start(bf16[2,256,256]{2,1,0:T(8,128)(2,1)} %param.27) | copy-start | bytes 786436
  92.8 10.1 %copy-start.8 = (bf16[2,256,256]{2,1,0:T(8,128)(2,1)S(1)}, bf16[2,256,256]{2,1,0:T(8,128)(2,1)}, u32[]{:S(2)}) copy-start(bf16[2,256,256]{2,1,0:T(8,128)(2,1)} %param.26) | copy-start | bytes 786436
  103.0 1.0 copy-start.3
